TPU v7x, 32 devices: a whole 2x2x4 slice. The times are simulated.
32 devices in a mesh: dp: 4 (over y, x), shard: 8 (over z, core).
Axes of the slice: x: 2, y: 2, z: 4, core: 2. Of those that a mesh axis runs over, the one named last changes fastest.
Arguments:
- id_table: float32 [262144, 128], P(('dp', 'shard')), may hold values from -6 to 6
- ada_state: float32 [262144], P(('dp', 'shard')), may hold values from 0.01 to 1
- user_first: float32 [128, 512], replicated, may hold values from -0.5 to 0.5
- user_second: float32 [512, 128], replicated, may hold values from -0.25 to 0.25
- item_first: float32 [128, 512], replicated, may hold values from -0.5 to 0.5
- item_second: float32 [512, 128], replicated, may hold values from -0.25 to 0.25
- fetch_rows: int32 [32, 4, 8, 72], P(('dp', 'shard')), may hold values from 0 to 8191
- lookup_slots: int32 [32, 1536], P(('dp', 'shard')), may hold values from 0 to 2303
Outputs:
- new_table: float32 [262144, 128], P(('dp', 'shard'))
- new_state: float32 [262144], P(('dp', 'shard'))
- user_first_grad: float32 [128, 512], replicated
- user_second_grad: float32 [512, 128], replicated
- item_first_grad: float32 [128, 512], replicated
- item_second_grad: float32 [512, 128], replicated
- mean_loss: float32 [], replicated
All inputs are finite; a program needn't handle non-finite values.
Results may differ from a plain program's by a relative error of at most 0.0038.
The roundings to bfloat16 on the way count: a program that leaves them out, or rounds other values in their place, can miss the bound.
Values may be sent and summed in bfloat16 or wider, within the bound.
No kernel may reach another device: no remote copies, remote signals or barrier semaphores. Data moves between devices by JAX's collectives and lax.ppermute only.
A program may use at most 128 MiB of HBM per device.

v0:
```python
import jax
import jax.numpy as jnp
from jax import lax
from jax.sharding import PartitionSpec as P

EXAMPLES_ON_CHIP = 512
highest = lax.Precision.HIGHEST
logit_divisor = 0.025
learn_rate = 0.1
epsilon = 1e-08


def tower_pass(looked, first_w, second_w):
    hidden_act = jax.nn.silu(
        jnp.dot(looked, first_w, precision=highest, preferred_element_type=jnp.float32)
    )
    tower_out = jnp.dot(hidden_act, second_w, precision=highest, preferred_element_type=jnp.float32)
    return tower_out / jnp.sqrt(jnp.sum(tower_out * tower_out, axis=1, keepdims=True) + 1e-06)


def score_block(user_half_precision, candidate_half_precision):
    return (
        jnp.dot(user_half_precision, candidate_half_precision.T, preferred_element_type=jnp.float32)
        / logit_divisor
    )


def cand_step(candidate_half_precision, user_half_precision):
    exponent = jnp.exp(score_block(user_half_precision, candidate_half_precision))
    collected_entries = jnp.dot(
        exponent.astype(jnp.bfloat16), candidate_half_precision, preferred_element_type=jnp.float32
    )
    return (jnp.sum(exponent, axis=1), collected_entries)


def item_term(user_half_precision, log_z, candidate_half_precision):
    softmax = jnp.exp(
        score_block(user_half_precision, candidate_half_precision) - log_z[:, None]
    ).astype(jnp.bfloat16)
    return jnp.dot(softmax.T, user_half_precision, preferred_element_type=jnp.float32)


def per_device(
    id_table, ada_state, user_first, user_second, item_first, item_second, fetch_rows, lookup_slots
):
    target_index_vector = id_table.shape[1]
    examples_on_chip = EXAMPLES_ON_CHIP
    asked_rows = lax.all_to_all(
        lax.all_to_all(fetch_rows[0], "dp", split_axis=0, concat_axis=0, tiled=True),
        "shard",
        split_axis=1,
        concat_axis=1,
        tiled=True,
    )
    fetched = jnp.take(id_table, asked_rows.reshape(-1), axis=0).reshape(
        asked_rows.shape + (target_index_vector,)
    )
    returned = lax.all_to_all(
        lax.all_to_all(fetched, "dp", split_axis=0, concat_axis=0, tiled=True),
        "shard",
        split_axis=1,
        concat_axis=1,
        tiled=True,
    )
    slot_rows = returned.reshape(-1, target_index_vector)
    slot_index = lookup_slots[0]
    looked = jnp.take(slot_rows, slot_index, axis=0)
    user_vec, user_pull = jax.vjp(tower_pass, looked[:examples_on_chip], user_first, user_second)
    item_vec, item_pull = jax.vjp(tower_pass, looked[examples_on_chip:], item_first, item_second)
    user_half_precision = user_vec.astype(jnp.bfloat16)
    item_bf = item_vec.astype(jnp.bfloat16)
    query_single_float = user_half_precision.astype(jnp.float32)
    resident_target_entries = item_bf[:examples_on_chip].astype(jnp.float32)
    matching_pair_logit = (
        jnp.sum(query_single_float * resident_target_entries, axis=1) / logit_divisor
    )
    reduced_aggregates, collected_entries = cand_step(
        lax.all_gather(item_bf, "dp", axis=0, tiled=True), user_half_precision
    )
    log_z = jnp.log(reduced_aggregates)
    target_derivative_accrual = item_term(
        lax.all_gather(user_vec, "dp", axis=0, tiled=True).astype(jnp.bfloat16),
        lax.all_gather(log_z, "dp", axis=0, tiled=True),
        item_bf,
    )
    query_adjoint = (
        collected_entries / reduced_aggregates[:, None] - resident_target_entries
    ) / logit_divisor
    target_adjoint = (
        target_derivative_accrual.at[:examples_on_chip].add(-query_single_float) / logit_divisor
    )
    user_look, user_first_g, user_second_g = user_pull(query_adjoint)
    item_look, item_first_g, item_second_g = item_pull(target_adjoint)
    look_grads = jnp.concatenate([user_look, item_look], axis=0)
    slot_grads = jnp.zeros_like(slot_rows).at[slot_index].add(look_grads)
    sent_back = lax.all_to_all(
        lax.all_to_all(
            slot_grads.reshape(returned.shape).astype(jnp.bfloat16),
            "dp",
            split_axis=0,
            concat_axis=0,
            tiled=True,
        ),
        "shard",
        split_axis=1,
        concat_axis=1,
        tiled=True,
    ).astype(jnp.float32)
    grad_rows = (
        jnp.zeros_like(id_table)
        .at[asked_rows.reshape(-1)]
        .add(sent_back.reshape(-1, target_index_vector))
    )
    new_state = ada_state + jnp.mean(grad_rows * grad_rows, axis=1)
    new_table = id_table - learn_rate * grad_rows / (jnp.sqrt(new_state)[:, None] + epsilon)
    loss_part = jnp.sum(log_z - matching_pair_logit)
    summed = lax.psum(
        (user_first_g, user_second_g, item_first_g, item_second_g, loss_part), ("dp", "shard")
    )
    shard_number = lax.axis_size("dp") * lax.axis_size("shard")
    return (
        new_table,
        new_state,
        summed[0] / shard_number,
        summed[1] / shard_number,
        summed[2] / shard_number,
        summed[3] / shard_number,
        summed[4] / (shard_number * examples_on_chip),
    )


def solution(mesh):
    return jax.shard_map(
        per_device,
        mesh=mesh,
        in_specs=(
            P(("dp", "shard"), None),
            P(("dp", "shard")),
            P(),
            P(),
            P(),
            P(),
            P(("dp", "shard"), None, None, None),
            P(("dp", "shard"), None),
        ),
        out_specs=(P(("dp", "shard"), None), P(("dp", "shard")), P(), P(), P(), P(), P()),
        check_vma=False,
    )
```

profile of v0, /device:TPU:0, one launch (start us, length us, event | category | flops | bytes accessed | tf_op | source)
XLA Modules:
  0.0 361.9 jit_solution(15782953325688524731)
XLA Ops:
  7.2 10.0 %all_to_all.30 = s32[4,8,72]{2,1,0:T(8,128)S(1)} all-to-all(s32[4,8,72]{2,1,0:T(8,128)} %bitcast.34), channel_id=1, replica_groups=mesh['dp'=4,'shard'=8] {'dp'}, dimensions={0} | all-to-all | bytes 18432 | tf_op jit(solution)/shard_map/all_to_all | solution.py:49
  17.2 10.3 %all_to_all.31 = s32[4,8,72]{2,0,1:T(4,128)S(1)} all-to-all(s32[4,8,72]{2,0,1:T(4,128)S(1)} %copy.24), channel_id=1, replica_groups=mesh['dp'=4,'shard'=8] {'shard'}, dimensions={1} | all-to-all | bytes 18432 | tf_op jit(solution)/shard_map/all_to_all | solution.py:48
  28.3 6.1 %gather_fusion = f32[2304,128]{1,0:T(8,128)S(1)} fusion(f32[8192,128]{1,0:T(8,128)} %param.10, s32[3072]{0:T(1024)S(1)} %pad_clamp_fusion), kind=kCustom, calls=%fused_computation | custom fusion | bytes 2368512 | tf_op jit(solution)/shard_map/jit(_take)/gather | solution.py:55
  34.9 18.2 %all_to_all.32 = f32[4,8,72,128]{3,2,1,0:T(8,128)S(1)} all-to-all(f32[4,8,72,128]{3,2,1,0:T(8,128)S(1)} %broadcast_select_fusion), channel_id=1, replica_groups=mesh['dp'=4,'shard'=8] {'dp'}, dimensions={0} | all-to-all | bytes 2359296 | tf_op jit(solution)/shard_map/all_to_all | solution.py:59
  54.2 3.6 all-to-all-start.3
  57.9 29.1 %all-to-all-done.3 = f32[4,8,72,128]{3,2,0,1:T(8,128)S(1)} async-done(((f32[4,8,72,128]{3,2,0,1:T(8,128)}), f32[4,8,72,128]{3,2,0,1:T(8,128)S(1)}, u32[]{:S(2)}, u32[]{:S(2)}) %all-to-all-start.3) | async-done | bytes 1179680 | tf_op jit(solution)/shard_map/all_to_all | solution.py:58
  91.9 2.7 multiply_reduce_fusion.2
  97.3 2.7 multiply_reduce_fusion.4
  101.3 11.5 %all_gather.10 = bf16[2048,128]{0,1:T(8,128)(2,1)} all-gather(bf16[512,128]{0,1:T(8,128)(2,1)S(1)} %get-tuple-element.24), channel_id=1, replica_groups=mesh['dp'=4,'shard'=8] {'dp'}, dimensions={0}, use_global_device_ids=true | all-gather | bytes 655360 | tf_op jit(solution)/shard_map/all_gather | solution.py:82
  112.8 8.4 %all-gather.3.cloned.1.call-done = bf16[4096,128]{0,1:T(8,128)(2,1)} async-done(((bf16[1024,128]{0,1:T(8,128)(2,1)}), bf16[4096,128]{0,1:T(8,128)(2,1)}) %all-gather.3.cloned.1.call-update) | async-done | bytes 1048592 | tf_op jit(solution)/shard_map/all_gather | solution.py:78
  121.2 5.8 %fusion = (f32[512]{0:T(512)S(1)}, f32[512,4096]{1,0:T(8,128)}) fusion(bf16[512,128]{0,1:T(8,128)(2,1)S(1)} %get-tuple-element.24, bf16[4096,128]{0,1:T(8,128)(2,1)} %all-gather.3.cloned.1.call-done), kind=kOutput, calls=%fused_computation.6 | convolution fusion | flops 541064704 | bytes 9570304 | tf_op jit(solution)/shard_map/dot_general | solution.py:23
  127.6 8.8 %all-gather = f32[4,1,512]{2,1,0:T(1,128)} all-gather(f32[1,1,512]{2,1,0:T(1,128)S(1)} %bitcast.36), channel_id=1, replica_groups=mesh['dp'=4,'shard'=8] {'dp'}, dimensions={0}, use_global_device_ids=true | all-gather | bytes 10240 | tf_op jit(solution)/shard_map/all_gather | solution.py:83
  136.5 4.1 %fusion.10 = f32[1024,128]{0,1:T(8,128)} fusion(bf16[1024,128]{0,1:T(8,128)(2,1)S(1)} %copy-done.3, f32[2048]{0:T(1024)} %bitcast.35, bf16[2048,128]{0,1:T(8,128)(2,1)} %all_gather.10), kind=kOutput, calls=%fused_computation.19 | convolution fusion | flops 1080033280 | bytes 1318912 | tf_op jit(solution)/shard_map/dot_general | solution.py:40
  144.6 3.8 %fusion.6 = f32[1024,512]{1,0:T(8,128)S(1)} fusion(f32[1024,512]{1,0:T(8,128)S(1)} %fusion.30, f32[512,128]{1,0:T(8,128)S(1)} %copy-done, f32[1024,128]{0,1:T(8,128)} %copy-done.5, f32[1024,128]{0,1:T(8,128)} %fusion.37, f32[1024]{0:T(1024)S(1)} %multiply_multiply_fusion, f32[1024]{0:T(1024)} %copy-done.17), kind=kOutput, calls=%fused_computation.14 | convolution fusion | flops 810680320 | bytes 5513216 | tf_op jit(solution)/shard_map/transpose(jvp())/dot_general | solution.py:17
  154.8 2.6 fusion.43
  160.0 9.3 %scatter_custom_fusion = f32[2304,128]{1,0:T(8,128)S(1)} fusion(s32[1536]{0:T(1024)S(1)} %fusion.48, f32[1024,128]{1,0:T(8,128)} %fusion.58, f32[]{:T(128)} %constant.111, f32[512,128]{1,0:T(8,128)S(1)} %fusion.57, f32[]{:T(128)} %constant.90.clone.1), kind=kCustom, calls=%fused_computation.28 | custom fusion | flops 393216 | bytes 1966088 | tf_op jit(solution)/shard_map/scatter-add | solution.py:95
  170.2 3.5 all-to-all-start.4
  173.7 6.2 %fusion.32 = f32[512,128]{1,0:T(8,128)} fusion(f32[1024,512]{1,0:T(8,128)} %copy-done.4, f32[1024,128]{0,1:T(8,128)} %copy-done.5, f32[1024,128]{0,1:T(8,128)} %fusion.37, f32[1024]{0:T(1024)S(1)} %copy-done.26, f32[1024]{0:T(1024)S(1)} %copy-done.18), kind=kOutput, calls=%fused_computation.45 | convolution fusion | flops 808058880 | bytes 3416064 | tf_op jit(solution)/shard_map/transpose(jvp())/dot_general | solution.py:17
  181.5 4.6 %all-to-all-start.5 = ((bf16[4,8,72,128]{3,2,0,1:T(8,128)(2,1)}), bf16[4,8,72,128]{3,2,0,1:T(8,128)(2,1)S(1)}, u32[]{:S(2)}, u32[]{:S(2)}) async-start(bf16[4,8,72,128]{3,2,0,1:T(8,128)(2,1)} %copy.29), calls=%async_computation.5 | async-start | bytes 1179648 | tf_op jit(solution)/shard_map/all_to_all | solution.py:96
  187.7 40.8 %psum.39 = f32[]{:T(128)} all-reduce(f32[]{:T(128)} %get-tuple-element.29), channel_id=1, replica_groups=mesh['dp'=4,'shard'=8] {'dp','shard'}, use_global_device_ids=true, to_apply=%region_14.15 | all-reduce | flops 1 | bytes 8 | tf_op jit(solution)/shard_map/psum | solution.py:117
  229.1 96.8 %all-reduce.3.cloned.1.call-done = (f32[128,512]{1,0:T(8,128)}, f32[512,128]{1,0:T(8,128)}, f32[128,512]{1,0:T(8,128)}, f32[512,128]{1,0:T(8,128)}) async-done(((f32[128,512]{1,0:T(8,128)}, f32[512,128]{1,0:T(8,128)}, f32[128,512]{1,0:T(8,128)}, f32[512,128]{1,0:T(8,128)}), (f32[128,512]{1,0:T(8,128)}, f32[512,128]{1,0:T(8,128)}, f32[128,512]{1,0:T(8,128)}, ...) | async-done | bytes 1048592 | tf_op jit(solution)/shard_map/psum | solution.py:117
  329.8 15.8 %scatter_custom_fusion.1 = f32[8192,128]{1,0:T(8,128)} fusion(s32[2304]{0:T(1024)} %copy-done.14, f32[]{:T(128)} %constant.90.clone.1, bf16[2304,128]{1,0:T(8,128)(2,1)S(1)} %bitcast.32), kind=kCustom, calls=%fused_computation.17 | custom fusion | flops 589824 | bytes 4784640 | tf_op jit(solution)/shard_map/scatter-add | solution.py:112
  345.6 3.5 multiply_reduce_fusion
  349.7 4.2 %divide_subtract_fusion = f32[8192,128]{1,0:T(8,128)} fusion(f32[8192,128]{1,0:T(8,128)S(1)} %copy-done.1, f32[8192,128]{1,0:T(8,128)} %scatter_custom_fusion.1, f32[8192]{0:T(1024)S(1)} %get-tuple-element.25), kind=kLoop, calls=%fused_computation.9 | loop fusion | flops 3145728 | bytes 12615680 | tf_op jit(solution)/shard_map/sub | solution.py:115
  (106 shorter events, 32.9 us)
Async XLA Ops:
  7.2 84.7 %copy-start = (f32[512,128]{1,0:T(8,128)S(1)}, f32[512,128]{1,0:T(8,128)}, u32[]{:S(2)}) copy-start(f32[512,128]{1,0:T(8,128)} %param.15) | copy-start | bytes 786436
  53.1 4.7 %copy-start.16 = (s32[1,1536]{1,0:T(1,128)S(1)}, s32[1,1536]{1,0:T(1,128)}, u32[]{:S(2)}) copy-start(s32[1,1536]{1,0:T(1,128)} %param.17) | copy-start | bytes 18436
  54.2 32.9 %all-to-all-start.3 = ((f32[4,8,72,128]{3,2,0,1:T(8,128)}), f32[4,8,72,128]{3,2,0,1:T(8,128)S(1)}, u32[]{:S(2)}, u32[]{:S(2)}) async-start(f32[4,8,72,128]{3,2,0,1:T(8,128)} %copy.27), calls=%async_computation.3 | async-start | bytes 2359296 | tf_op jit(solution)/shard_map/all_to_all | solution.py:58
  57.8 63.4 %all-gather.3.cloned.1.call-start = ((), (), s32[]{:S(2)}) async-start(), calls=%async_computation.6 | async-start | bytes 1310720 | tf_op jit(solution)/shard_map/all_gather | solution.py:78
  87.2 2.9 copy-start.12
  91.9 52.7 %copy-start.4 = (f32[1024,512]{1,0:T(8,128)}, f32[1024,512]{1,0:T(8,128)S(1)}, u32[]{:S(2)}) copy-start(f32[1024,512]{1,0:T(8,128)S(1)} %fusion.30) | copy-start | bytes 6291460
  91.9 4.3 %copy-start.10 = (f32[128,512]{1,0:T(8,128)S(1)}, f32[128,512]{1,0:T(8,128)}, u32[]{:S(2)}) copy-start(f32[128,512]{1,0:T(8,128)} %param.12) | copy-start | bytes 786436
  94.7 5.3 %copy-start.19 = (f32[1024]{0:T(1024)}, f32[1024]{0:T(1024)S(1)}, u32[]{:S(2)}) copy-start(f32[1024]{0:T(1024)S(1)} %get-tuple-element.33) | copy-start | bytes 12292
  95.4 4.6 %copy-start.17 = (f32[1024]{0:T(1024)}, f32[1024]{0:T(1024)S(1)}, u32[]{:S(2)}) copy-start(f32[1024]{0:T(1024)S(1)} %get-tuple-element.28) | copy-start | bytes 12292
  97.2 2.7 copy-start.8
  97.2 3.4 copy-start.3
  100.0 12.9 %copy-start.20 = (f32[512]{0:T(512)}, f32[512]{0:T(512)S(1)}, u32[]{:S(2)}) copy-start(f32[512]{0:T(512)S(1)} %get-tuple-element.32) | copy-start | bytes 6148
  121.2 5.8 %copy-start.22 = (f32[512]{0:T(512)S(1)}, f32[512]{0:T(512)}, u32[]{:S(2)}) copy-start(f32[512]{0:T(512)} %get-tuple-element.23) | copy-start | bytes 6148
  142.3 10.8 %slice-start = ((s8[8388608]{0:T(1024)(128)(4,1)}), s8[4194304]{0:T(1024)(128)(4,1)S(1)}, s32[]{:S(2)}) async-start(s8[8388608]{0:T(1024)(128)(4,1)} %bitcast.28), calls=%async_computation.8 | async-start | bytes 8388608
  144.6 3.8 %copy-start.25 = (f32[1024]{0:T(1024)}, f32[1024]{0:T(1024)S(1)}, u32[]{:S(2)}) copy-start(f32[1024]{0:T(1024)S(1)} %multiply_multiply_fusion) | copy-start | bytes 12292
  144.6 8.5 %slice-start.1 = ((s8[8388608]{0:T(1024)(128)(4,1)}), s8[4194304]{0:T(1024)(128)(4,1)S(1)}, s32[]{:S(2)}) async-start(s8[8388608]{0:T(1024)(128)(4,1)} %bitcast.28), calls=%async_computation.9 | async-start | bytes 8388608
  154.8 2.6 copy-start.27
  160.0 13.7 %copy-start.18 = (f32[1024]{0:T(1024)S(1)}, f32[1024]{0:T(1024)}, u32[]{:S(2)}) copy-start(f32[1024]{0:T(1024)} %copy-done.17) | copy-start | bytes 12292
  160.0 13.7 %copy-start.26 = (f32[1024]{0:T(1024)S(1)}, f32[1024]{0:T(1024)}, u32[]{:S(2)}) copy-start(f32[1024]{0:T(1024)} %copy-done.25) | copy-start | bytes 12292
  170.2 10.4 %all-to-all-start.4 = ((bf16[4,8,72,128]{3,2,1,0:T(8,128)(2,1)}), bf16[4,8,72,128]{3,2,1,0:T(8,128)(2,1)S(1)}, u32[]{:S(2)}, u32[]{:S(2)}) async-start(bf16[4,8,72,128]{3,2,1,0:T(8,128)(2,1)} %bitcast.33), calls=%async_computation.4 | async-start | bytes 1179648 | tf_op jit(solution)/shard_map/all_to_all | solution.py:97
  181.5 148.2 %all-to-all-start.5 = ((bf16[4,8,72,128]{3,2,0,1:T(8,128)(2,1)}), bf16[4,8,72,128]{3,2,0,1:T(8,128)(2,1)S(1)}, u32[]{:S(2)}, u32[]{:S(2)}) async-start(bf16[4,8,72,128]{3,2,0,1:T(8,128)(2,1)} %copy.29), calls=%async_computation.5 | async-start | bytes 1179648 | tf_op jit(solution)/shard_map/all_to_all | solution.py:96
  186.1 139.9 %all-reduce.3.cloned.1.call-start = ((), (), s32[]{:S(2)}) async-start(), calls=%async_computation.7 | async-start | bytes 2097152 | tf_op jit(solution)/shard_map/psum | solution.py:117
  345.6 3.5 copy-start.15
  345.6 4.1 %copy-start.1 = (f32[8192,128]{1,0:T(8,128)S(1)}, f32[8192,128]{1,0:T(8,128)}, u32[]{:S(2)}) copy-start(f32[8192,128]{1,0:T(8,128)} %param.10) | copy-start | bytes 12582916
  (11 other events, 16.5 us)
Sparse Core Ops, SparseCore 0:
  96.4 24.8 all-gather.2
  193.0 132.9 all-reduce.2
where the time goes:
time: 363 us; the launch traced here: 362 us
  waiting for transfers between devices  135 us (37%)
  blocking collectives  99.8 us (27%)
  other arithmetic  45.6 us (13%)
  matrix products  41 us (11%)
  between operations  16.3 us (4%)
  local copies, waits for them, and re-layouts  12.4 us (3%)
  starting transfers between devices  11.7 us (3%)
    psum x1, waiting for transfers between devices, per_device(): lax.psum((user_first_g, user_second_g, item_first_g, item_second_g, loss_...  96.8 us
    psum x1, blocking collectives, per_device(): lax.psum((user_first_g, user_second_g, item_first_g, item_second_g, loss_...  40.8 us
    all_to_all x1, waiting for transfers between devices, per_device(): lax.all_to_all(lax.all_to_all(fetched, 'dp', split_axis=0, concat_axis=0,...  29.1 us
    dot_general x6, matrix products, tower_pass(): jnp.dot(hidden_act, second_w, precision=highest, preferred_element_type=j...  19.6 us
    all_to_all x1, blocking collectives, per_device(): lax.all_to_all(fetched, 'dp', split_axis=0, concat_axis=0, tiled=True)  18.2 us
    scatter-add x1, other arithmetic, per_device(): grad_rows = jnp.zeros_like(id_table).at[asked_rows.reshape(-1)].add(sent_...  15.8 us
    all_gather x1, blocking collectives, per_device(): lax.all_gather(user_vec, 'dp', axis=0, tiled=True).astype(jnp.bfloat16)  11.5 us
    all_to_all x1, blocking collectives, per_device(): lax.all_to_all(lax.all_to_all(fetch_rows[0], 'dp', split_axis=0, concat_a...  10.3 us
  transfers between devices with their start and end apart: 5, of which 4 were waited for; matrix products, arithmetic and copies ran while one was open for 4% of the time, Pallas kernels for 0%

commit v1 on v0

--- a/solution.py
+++ b/solution.py
@@ -8,6 +8,12 @@
 logit_divisor = 0.025
 learn_rate = 0.1
 epsilon = 1e-08
+
+
+def exchange_blocks(array, axis, split, join):
+    pieces = jnp.split(array, lax.axis_size(axis), axis=split)
+    got = lax.all_to_all(jnp.stack(pieces), axis, 0, 0)
+    return jnp.concatenate(got, axis=join)
 
 
 def tower_pass(looked, first_w, second_w):
@@ -55,12 +61,8 @@
     fetched = jnp.take(id_table, asked_rows.reshape(-1), axis=0).reshape(
         asked_rows.shape + (target_index_vector,)
     )
-    returned = lax.all_to_all(
-        lax.all_to_all(fetched, "dp", split_axis=0, concat_axis=0, tiled=True),
-        "shard",
-        split_axis=1,
-        concat_axis=1,
-        tiled=True,
+    returned = exchange_blocks(
+        lax.all_to_all(fetched, "dp", split_axis=0, concat_axis=0, tiled=True), "shard", 1, 1
     )
     slot_rows = returned.reshape(-1, target_index_vector)
     slot_index = lookup_slots[0]

time: 363 us -> 367 us (1.011)
  local copies, waits for them, and re-layouts: 12.4 us -> 16.6 us
    unnamed x60 -> x67, local copies, waits for them, and re-layouts: 1.49 us -> 6.19 us
where the time goes in v1:
time: 367 us; the launch traced here: 366 us
  waiting for transfers between devices  135 us (37%)
  blocking collectives  99.7 us (27%)
  other arithmetic  45.6 us (12%)
  matrix products  41 us (11%)
  local copies, waits for them, and re-layouts  16.6 us (5%)
  between operations  16.3 us (4%)
  starting transfers between devices  11.7 us (3%)
    psum x1, waiting for transfers between devices, per_device(): lax.psum((user_first_g, user_second_g, item_first_g, item_second_g, loss_...  96.8 us
    psum x1, blocking collectives, per_device(): lax.psum((user_first_g, user_second_g, item_first_g, item_second_g, loss_...  40.8 us
    all_to_all x1, waiting for transfers between devices, exchange_blocks(): got = lax.all_to_all(jnp.stack(pieces), axis, 0, 0)  29.1 us
    dot_general x6, matrix products, tower_pass(): jnp.dot(hidden_act, second_w, precision=highest, preferred_element_type=j...  19.6 us
    all_to_all x1, blocking collectives, per_device(): lax.all_to_all(fetched, 'dp', split_axis=0, concat_axis=0, tiled=True)  18.2 us
    scatter-add x1, other arithmetic, per_device(): grad_rows = jnp.zeros_like(id_table).at[asked_rows.reshape(-1)].add(sent_...  15.8 us
    all_gather x1, blocking collectives, per_device(): lax.all_gather(user_vec, 'dp', axis=0, tiled=True).astype(jnp.bfloat16)  11.5 us
    all_to_all x1, blocking collectives, per_device(): lax.all_to_all(lax.all_to_all(fetch_rows[0], 'dp', split_axis=0, concat_a...  10.3 us
  transfers between devices with their start and end apart: 5, of which 4 were waited for; matrix products, arithmetic and copies ran while one was open for 4% of the time, Pallas kernels for 0%

profile of v1, /device:TPU:0, one launch (start us, length us, event | category | flops | bytes accessed | tf_op | source)
XLA Modules:
  0.0 366.1 jit_solution(4604862800508863876)
XLA Ops:
  7.2 10.0 %all_to_all.30 = s32[4,8,72]{2,1,0:T(8,128)S(1)} all-to-all(s32[4,8,72]{2,1,0:T(8,128)} %bitcast.82), channel_id=1, replica_groups=mesh['dp'=4,'shard'=8] {'dp'}, dimensions={0} | all-to-all | bytes 18432 | tf_op jit(solution)/shard_map/all_to_all | solution.py:55
  17.2 10.3 %all_to_all.31 = s32[4,8,72]{2,0,1:T(4,128)S(1)} all-to-all(s32[4,8,72]{2,0,1:T(4,128)S(1)} %copy.54), channel_id=1, replica_groups=mesh['dp'=4,'shard'=8] {'shard'}, dimensions={1} | all-to-all | bytes 18432 | tf_op jit(solution)/shard_map/all_to_all | solution.py:54
  28.3 6.1 %gather_fusion = f32[2304,128]{1,0:T(8,128)S(1)} fusion(f32[8192,128]{1,0:T(8,128)} %param.10, s32[3072]{0:T(1024)S(1)} %pad_clamp_fusion), kind=kCustom, calls=%fused_computation | custom fusion | bytes 2368512 | tf_op jit(solution)/shard_map/jit(_take)/gather | solution.py:61
  34.9 18.2 %all_to_all.32 = f32[4,8,72,128]{3,2,1,0:T(8,128)S(1)} all-to-all(f32[4,8,72,128]{3,2,1,0:T(8,128)S(1)} %broadcast_select_fusion), channel_id=1, replica_groups=mesh['dp'=4,'shard'=8] {'dp'}, dimensions={0} | all-to-all | bytes 2359296 | tf_op jit(solution)/shard_map/all_to_all | solution.py:65
  58.5 3.6 all-to-all-start.3
  62.2 29.1 %all-to-all-done.3 = f32[8,4,1,72,128]{4,3,1,2,0:T(8,128)S(1)} async-done(((f32[8,4,1,72,128]{4,3,1,2,0:T(8,128)}), f32[8,4,1,72,128]{4,3,1,2,0:T(8,128)S(1)}, u32[]{:S(2)}, u32[]{:S(2)}) %all-to-all-start.3) | async-done | bytes 1179680 | tf_op jit(solution)/shard_map/all_to_all | solution.py:15
  96.2 2.7 multiply_reduce_fusion.2
  101.5 2.7 multiply_reduce_fusion.4
  105.6 11.5 %all_gather.10 = bf16[2048,128]{0,1:T(8,128)(2,1)} all-gather(bf16[512,128]{0,1:T(8,128)(2,1)S(1)} %get-tuple-element.24), channel_id=1, replica_groups=mesh['dp'=4,'shard'=8] {'dp'}, dimensions={0}, use_global_device_ids=true | all-gather | bytes 655360 | tf_op jit(solution)/shard_map/all_gather | solution.py:84
  117.1 8.4 %all-gather.3.cloned.1.call-done = bf16[4096,128]{0,1:T(8,128)(2,1)} async-done(((bf16[1024,128]{0,1:T(8,128)(2,1)}), bf16[4096,128]{0,1:T(8,128)(2,1)}) %all-gather.3.cloned.1.call-update) | async-done | bytes 1048592 | tf_op jit(solution)/shard_map/all_gather | solution.py:80
  125.5 5.8 %fusion = (f32[512]{0:T(512)S(1)}, f32[512,4096]{1,0:T(8,128)}) fusion(bf16[512,128]{0,1:T(8,128)(2,1)S(1)} %get-tuple-element.24, bf16[4096,128]{0,1:T(8,128)(2,1)} %all-gather.3.cloned.1.call-done), kind=kOutput, calls=%fused_computation.6 | convolution fusion | flops 541064704 | bytes 9570304 | tf_op jit(solution)/shard_map/dot_general | solution.py:29
  131.9 8.8 %all-gather = f32[4,1,512]{2,1,0:T(1,128)} all-gather(f32[1,1,512]{2,1,0:T(1,128)S(1)} %bitcast.84), channel_id=1, replica_groups=mesh['dp'=4,'shard'=8] {'dp'}, dimensions={0}, use_global_device_ids=true | all-gather | bytes 10240 | tf_op jit(solution)/shard_map/all_gather | solution.py:85
  140.7 4.1 %fusion.10 = f32[1024,128]{0,1:T(8,128)} fusion(bf16[1024,128]{0,1:T(8,128)(2,1)S(1)} %copy-done.3, f32[2048]{0:T(1024)} %bitcast.83, bf16[2048,128]{0,1:T(8,128)(2,1)} %all_gather.10), kind=kOutput, calls=%fused_computation.19 | convolution fusion | flops 1080033280 | bytes 1318912 | tf_op jit(solution)/shard_map/dot_general | solution.py:46
  148.8 3.8 %fusion.6 = f32[1024,512]{1,0:T(8,128)S(1)} fusion(f32[1024,512]{1,0:T(8,128)S(1)} %fusion.30, f32[512,128]{1,0:T(8,128)S(1)} %copy-done, f32[1024,128]{0,1:T(8,128)} %copy-done.5, f32[1024,128]{0,1:T(8,128)} %fusion.37, f32[1024]{0:T(1024)S(1)} %multiply_multiply_fusion, f32[1024]{0:T(1024)} %copy-done.17), kind=kOutput, calls=%fused_computation.14 | convolution fusion | flops 810680320 | bytes 5513216 | tf_op jit(solution)/shard_map/transpose(jvp())/dot_general | solution.py:23
  159.0 2.6 fusion.43
  164.2 9.3 %scatter_custom_fusion = f32[2304,128]{1,0:T(8,128)S(1)} fusion(s32[1536]{0:T(1024)S(1)} %fusion.56, f32[1024,128]{1,0:T(8,128)} %fusion.66, f32[]{:T(128)} %constant.111, f32[512,128]{1,0:T(8,128)S(1)} %fusion.65, f32[]{:T(128)} %constant.90.clone.1), kind=kCustom, calls=%fused_computation.28 | custom fusion | flops 393216 | bytes 1966088 | tf_op jit(solution)/shard_map/scatter-add | solution.py:97
  174.5 3.5 all-to-all-start.4
  178.0 6.2 %fusion.32 = f32[512,128]{1,0:T(8,128)} fusion(f32[1024,512]{1,0:T(8,128)} %copy-done.4, f32[1024,128]{0,1:T(8,128)} %copy-done.5, f32[1024,128]{0,1:T(8,128)} %fusion.37, f32[1024]{0:T(1024)S(1)} %copy-done.26, f32[1024]{0:T(1024)S(1)} %copy-done.18), kind=kOutput, calls=%fused_computation.45 | convolution fusion | flops 808058880 | bytes 3416064 | tf_op jit(solution)/shard_map/transpose(jvp())/dot_general | solution.py:23
  185.8 4.6 %all-to-all-start.5 = ((bf16[4,8,72,128]{3,2,0,1:T(8,128)(2,1)}), bf16[4,8,72,128]{3,2,0,1:T(8,128)(2,1)S(1)}, u32[]{:S(2)}, u32[]{:S(2)}) async-start(bf16[4,8,72,128]{3,2,0,1:T(8,128)(2,1)} %copy.65), calls=%async_computation.5 | async-start | bytes 1179648 | tf_op jit(solution)/shard_map/all_to_all | solution.py:98
  191.9 40.8 %psum.39 = f32[]{:T(128)} all-reduce(f32[]{:T(128)} %get-tuple-element.29), channel_id=1, replica_groups=mesh['dp'=4,'shard'=8] {'dp','shard'}, use_global_device_ids=true, to_apply=%region_14.15 | all-reduce | flops 1 | bytes 8 | tf_op jit(solution)/shard_map/psum | solution.py:119
  233.4 96.8 %all-reduce.3.cloned.1.call-done = (f32[128,512]{1,0:T(8,128)}, f32[512,128]{1,0:T(8,128)}, f32[128,512]{1,0:T(8,128)}, f32[512,128]{1,0:T(8,128)}) async-done(((f32[128,512]{1,0:T(8,128)}, f32[512,128]{1,0:T(8,128)}, f32[128,512]{1,0:T(8,128)}, f32[512,128]{1,0:T(8,128)}), (f32[128,512]{1,0:T(8,128)}, f32[512,128]{1,0:T(8,128)}, f32[128,512]{1,0:T(8,128)}, ...) | async-done | bytes 1048592 | tf_op jit(solution)/shard_map/psum | solution.py:119
  334.0 15.8 %scatter_custom_fusion.1 = f32[8192,128]{1,0:T(8,128)} fusion(s32[2304]{0:T(1024)} %copy-done.14, f32[]{:T(128)} %constant.90.clone.1, bf16[2304,128]{1,0:T(8,128)(2,1)S(1)} %bitcast.80), kind=kCustom, calls=%fused_computation.17 | custom fusion | flops 589824 | bytes 4784640 | tf_op jit(solution)/shard_map/scatter-add | solution.py:114
  349.8 3.5 multiply_reduce_fusion
  354.0 4.2 %divide_subtract_fusion = f32[8192,128]{1,0:T(8,128)} fusion(f32[8192,128]{1,0:T(8,128)S(1)} %copy-done.1, f32[8192,128]{1,0:T(8,128)} %scatter_custom_fusion.1, f32[8192]{0:T(1024)S(1)} %get-tuple-element.25), kind=kLoop, calls=%fused_computation.9 | loop fusion | flops 3145728 | bytes 12615680 | tf_op jit(solution)/shard_map/sub | solution.py:117
  (113 shorter events, 37.2 us)
Async XLA Ops:
  7.2 89.0 %copy-start = (f32[512,128]{1,0:T(8,128)S(1)}, f32[512,128]{1,0:T(8,128)}, u32[]{:S(2)}) copy-start(f32[512,128]{1,0:T(8,128)} %param.15) | copy-start | bytes 786436
  54.5 7.7 %copy-start.16 = (s32[1,1536]{1,0:T(1,128)S(1)}, s32[1,1536]{1,0:T(1,128)}, u32[]{:S(2)}) copy-start(s32[1,1536]{1,0:T(1,128)} %param.17) | copy-start | bytes 18436
  58.5 32.9 %all-to-all-start.3 = ((f32[8,4,1,72,128]{4,3,1,2,0:T(8,128)}), f32[8,4,1,72,128]{4,3,1,2,0:T(8,128)S(1)}, u32[]{:S(2)}, u32[]{:S(2)}) async-start(f32[8,4,1,72,128]{4,3,1,2,0:T(8,128)} %fusion.47), calls=%async_computation.3 | async-start | bytes 2359296 | tf_op jit(solution)/shard_map/all_to_all | solution.py:15
  62.1 63.4 %all-gather.3.cloned.1.call-start = ((), (), s32[]{:S(2)}) async-start(), calls=%async_computation.6 | async-start | bytes 1310720 | tf_op jit(solution)/shard_map/all_gather | solution.py:80
  91.4 2.9 copy-start.12
  96.2 52.7 %copy-start.4 = (f32[1024,512]{1,0:T(8,128)}, f32[1024,512]{1,0:T(8,128)S(1)}, u32[]{:S(2)}) copy-start(f32[1024,512]{1,0:T(8,128)S(1)} %fusion.30) | copy-start | bytes 6291460
  96.2 4.3 %copy-start.10 = (f32[128,512]{1,0:T(8,128)S(1)}, f32[128,512]{1,0:T(8,128)}, u32[]{:S(2)}) copy-start(f32[128,512]{1,0:T(8,128)} %param.12) | copy-start | bytes 786436
  98.9 5.3 %copy-start.19 = (f32[1024]{0:T(1024)}, f32[1024]{0:T(1024)S(1)}, u32[]{:S(2)}) copy-start(f32[1024]{0:T(1024)S(1)} %get-tuple-element.33) | copy-start | bytes 12292
  99.6 4.6 %copy-start.17 = (f32[1024]{0:T(1024)}, f32[1024]{0:T(1024)S(1)}, u32[]{:S(2)}) copy-start(f32[1024]{0:T(1024)S(1)} %get-tuple-element.28) | copy-start | bytes 12292
  101.5 2.7 copy-start.8
  101.5 3.4 copy-start.3
  104.3 12.9 %copy-start.20 = (f32[512]{0:T(512)}, f32[512]{0:T(512)S(1)}, u32[]{:S(2)}) copy-start(f32[512]{0:T(512)S(1)} %get-tuple-element.32) | copy-start | bytes 6148
  125.5 5.8 %copy-start.22 = (f32[512]{0:T(512)S(1)}, f32[512]{0:T(512)}, u32[]{:S(2)}) copy-start(f32[512]{0:T(512)} %get-tuple-element.23) | copy-start | bytes 6148
  146.5 10.8 %slice-start = ((s8[8388608]{0:T(1024)(128)(4,1)}), s8[4194304]{0:T(1024)(128)(4,1)S(1)}, s32[]{:S(2)}) async-start(s8[8388608]{0:T(1024)(128)(4,1)} %bitcast.75), calls=%async_computation.8 | async-start | bytes 8388608
  148.8 3.8 %copy-start.25 = (f32[1024]{0:T(1024)}, f32[1024]{0:T(1024)S(1)}, u32[]{:S(2)}) copy-start(f32[1024]{0:T(1024)S(1)} %multiply_multiply_fusion) | copy-start | bytes 12292
  148.8 8.5 %slice-start.1 = ((s8[8388608]{0:T(1024)(128)(4,1)}), s8[4194304]{0:T(1024)(128)(4,1)S(1)}, s32[]{:S(2)}) async-start(s8[8388608]{0:T(1024)(128)(4,1)} %bitcast.75), calls=%async_computation.9 | async-start | bytes 8388608
  159.0 2.6 copy-start.27
  164.2 13.7 %copy-start.18 = (f32[1024]{0:T(1024)S(1)}, f32[1024]{0:T(1024)}, u32[]{:S(2)}) copy-start(f32[1024]{0:T(1024)} %copy-done.17) | copy-start | bytes 12292
  164.2 13.7 %copy-start.26 = (f32[1024]{0:T(1024)S(1)}, f32[1024]{0:T(1024)}, u32[]{:S(2)}) copy-start(f32[1024]{0:T(1024)} %copy-done.25) | copy-start | bytes 12292
  174.5 10.4 %all-to-all-start.4 = ((bf16[4,8,72,128]{3,2,1,0:T(8,128)(2,1)}), bf16[4,8,72,128]{3,2,1,0:T(8,128)(2,1)S(1)}, u32[]{:S(2)}, u32[]{:S(2)}) async-start(bf16[4,8,72,128]{3,2,1,0:T(8,128)(2,1)} %bitcast.81), calls=%async_computation.4 | async-start | bytes 1179648 | tf_op jit(solution)/shard_map/all_to_all | solution.py:99
  185.8 148.2 %all-to-all-start.5 = ((bf16[4,8,72,128]{3,2,0,1:T(8,128)(2,1)}), bf16[4,8,72,128]{3,2,0,1:T(8,128)(2,1)S(1)}, u32[]{:S(2)}, u32[]{:S(2)}) async-start(bf16[4,8,72,128]{3,2,0,1:T(8,128)(2,1)} %copy.65), calls=%async_computation.5 | async-start | bytes 1179648 | tf_op jit(solution)/shard_map/all_to_all | solution.py:98
  190.4 139.9 %all-reduce.3.cloned.1.call-start = ((), (), s32[]{:S(2)}) async-start(), calls=%async_computation.7 | async-start | bytes 2097152 | tf_op jit(solution)/shard_map/psum | solution.py:119
  349.8 3.5 copy-start.15
  349.8 4.1 %copy-start.1 = (f32[8192,128]{1,0:T(8,128)S(1)}, f32[8192,128]{1,0:T(8,128)}, u32[]{:S(2)}) copy-start(f32[8192,128]{1,0:T(8,128)} %param.10) | copy-start | bytes 12582916
  (11 other events, 16.5 us)
Sparse Core Ops, SparseCore 0:
  100.6 24.7 all-gather.2
  197.3 132.9 all-reduce.2
